TPU v7x, 512 devices: a whole 4x8x8 slice. The times are simulated.
512 devices in a mesh: dp: 64 (over y, x, core), tensor: 8 (over z).
Axes of the slice: x: 4, y: 8, z: 8, core: 2. Of those that a mesh axis runs over, the one named last changes fastest.
Arguments:
- hidden_act: bfloat16 [32768, 1408], P('dp', 'tensor'), may hold values from -6 to 6
- cotangent: bfloat16 [32768, 2048], P('dp', 'tensor'), may hold values from -4 to 4
- down_table: bfloat16 [1408, 64, 2048], P('tensor', 'dp'), may hold values from -0.15625 to 0.15625
- expert_ids: int32 [128, 4], P('dp'), may hold values from 0 to 31, as said below
- merge_weights: float32 [128, 4], P('dp'), may hold values from 0.1 to 1
- owner_slot: int32 [32], replicated, may hold values from 0 to 63, as said below
Outputs:
- layer_out: bfloat16 [32768, 2048], P('dp', 'tensor')
- grad_hidden: bfloat16 [32768, 1408], P('dp', 'tensor')
- expert_grad: float32 [1408, 64, 2048], P('tensor', 'dp')
Inputs may be any that keep to these rules, and one draw needn't show every extreme that they name: `expert_ids`: each segment lists 4 different experts; the 2 segments of one index of dp list exactly 6 different experts together. `owner_slot`: different experts have different slots; slot 63 always holds an expert.
All inputs are finite; a program needn't handle non-finite values.
Results may differ from a plain program's by a relative error of at most 0.013.
Values may be sent and summed in bfloat16 or wider, within the bound.
A program may use at most 128 MiB of HBM per device.

v0:
```python
import jax
import jax.numpy as jnp
from jax import lax
from jax.sharding import PartitionSpec as P

E = 32
K = 4
POOL = 6


def pool_members(id_rows):
    listed = id_rows.reshape(-1)
    experts = jnp.arange(E, dtype=jnp.int32)
    present = jnp.any(listed[None, :] == experts[:, None], axis=1)
    ranking = jnp.cumsum(present.astype(jnp.int32)) - 1
    places = jnp.arange(POOL, dtype=jnp.int32)
    chosen = present[None, :] & (ranking[None, :] == places[:, None])
    return jnp.sum(jnp.where(chosen, experts[None, :], 0), axis=1)


def merge_coefficients(id_rows, weight_rows, targets):
    matches = id_rows[:, :, None] == targets[None, None, :]
    return jnp.sum(jnp.where(matches, weight_rows[:, :, None], 0.0), axis=1)


def body(hidden_act, cotangent, down_table, expert_ids, merge_weights, owner_slot):
    dp_count = lax.axis_size("dp")
    seg_count = expert_ids.shape[0]
    ff_local, slot_local, width = down_table.shape
    stripe = width // dp_count
    row_count = hidden_act.shape[0]
    seg_len = row_count // seg_count
    every_expert = jnp.arange(E, dtype=jnp.int32)
    all_ids, all_weights = (
        lax.all_gather(expert_ids, "dp", axis=0, tiled=True),
        lax.all_gather(merge_weights, "dp", axis=0, tiled=True),
    )
    ids_by_dev = all_ids.reshape(dp_count, seg_count, K)
    weights_by_dev = all_weights.reshape(dp_count, seg_count, K)
    pools_all = jax.vmap(pool_members)(ids_by_dev)
    my_pool = pools_all[lax.axis_index("dp")]
    my_coef = merge_coefficients(expert_ids, merge_weights, my_pool)
    member_table = (pools_all.T[:, :, None] == every_expert[None, None, :]).astype(jnp.bfloat16)
    stripes = lax.all_to_all(down_table, "dp", split_axis=2, concat_axis=1, tiled=True)
    by_expert = jnp.take(stripes, owner_slot, axis=1)
    outgoing = jnp.take(by_expert, pools_all.T, axis=1).reshape(ff_local, POOL, width)
    panel_set = lax.all_to_all(outgoing, "dp", split_axis=2, concat_axis=2, tiled=True)
    merged = jnp.sum(
        panel_set[:, None, :, :].astype(jnp.float32) * my_coef[None, :, :, None], axis=2
    ).astype(jnp.bfloat16)
    hidden_seg = hidden_act.reshape(seg_count, seg_len, ff_local)
    partial_rows = jnp.einsum(
        "stf,fsd->std", hidden_seg, merged, preferred_element_type=jnp.float32
    ).reshape(row_count, width)
    layer_out = lax.psum_scatter(
        partial_rows.astype(jnp.bfloat16), "tensor", scatter_dimension=1, tiled=True
    )
    full_cot = lax.all_gather(cotangent, "tensor", axis=1, tiled=True)
    cot_seg = full_cot.reshape(seg_count, seg_len, width)
    grad_hidden = (
        jnp.einsum("std,fsd->stf", cot_seg, merged, preferred_element_type=jnp.float32)
        .astype(jnp.bfloat16)
        .reshape(row_count, ff_local)
    )
    seg_grads = jnp.einsum(
        "stf,std->fsd", hidden_seg, cot_seg, preferred_element_type=jnp.float32
    ).astype(jnp.bfloat16)
    returned = lax.all_to_all(seg_grads, "dp", split_axis=2, concat_axis=2, tiled=True).reshape(
        ff_local, seg_count, dp_count, stripe
    )
    pool_coef = jax.vmap(merge_coefficients)(ids_by_dev, weights_by_dev, pools_all)
    coef_view = jnp.transpose(pool_coef, (1, 2, 0))
    group_sums = jnp.sum(
        returned[:, :, None, :, :].astype(jnp.float32) * coef_view[None, :, :, :, None], axis=1
    ).astype(jnp.bfloat16)
    grad_stripes = jnp.einsum(
        "fprd,pre->fed", group_sums, member_table, preferred_element_type=jnp.float32
    )
    slotted = (
        jnp.zeros((ff_local, slot_local * dp_count, stripe), jnp.float32)
        .at[:, owner_slot, :]
        .set(grad_stripes)
    )
    expert_grad = lax.all_to_all(
        slotted.astype(jnp.bfloat16), "dp", split_axis=1, concat_axis=2, tiled=True
    ).astype(slotted.dtype)
    return (layer_out, grad_hidden, expert_grad)


def solution(mesh):
    placed = (
        P("dp", "tensor"),
        P("dp", "tensor"),
        P("tensor", "dp", None),
        P("dp", None),
        P("dp", None),
        P(),
    )
    return jax.shard_map(
        body,
        mesh=mesh,
        in_specs=placed,
        out_specs=(P("dp", "tensor"), P("dp", "tensor"), P("tensor", "dp", None)),
        check_vma=False,
    )
```

profile of v0, /device:TPU:1, one launch (start us, length us, event | category | flops | bytes accessed | tf_op | source)
XLA Modules:
  0.0 478.6 jit_solution(9711148216334973201)
XLA Ops:
  7.2 4.5 copy.81
  11.7 0.5 broadcast.42
  12.2 11.6 %reduce.2 = bf16[2048,176]{1,0:T(8,128)(2,1)S(1)} reduce(bf16[2048,1,176]{2,1,0:T(2,128)(2,1)S(1)} %bitcast.55, bf16[]{:T(256)} %broadcast.42), dimensions={1}, to_apply=%bitcast.44.reduce_sub_computation | reduce | bytes 1441794
  23.9 0.0 copy-start.4
  23.9 0.0 copy-start.6
  23.9 2.6 reshape.124
  26.5 11.6 %all-to-all-start = ((bf16[64,2,2816]{2,1,0:T(2,128)(2,1)}), bf16[64,2,2816]{2,1,0:T(2,128)(2,1)S(1)}, u32[]{:S(2)}, u32[]{:S(2)}) async-start(bf16[64,2,2816]{2,1,0:T(2,128)(2,1)} %reshape.124), calls=%async_computation | async-start | bytes 1441792 | tf_op jit(solution)/shard_map/all_to_all | solution.py:44
  38.1 0.0 copy-done.4
  38.1 50.6 %all-gather = s32[64,2,4]{2,1,0:T(2,128)S(1)} all-gather(s32[1,2,4]{2,1,0:T(2,128)S(1)} %bitcast.65), channel_id=1, replica_groups=mesh['dp'=64,'tensor'=8] {'dp'}, dimensions={0}, use_global_device_ids=true | all-gather | bytes 2080 | tf_op jit(solution)/shard_map/all_gather | solution.py:35
  88.8 0.1 copy.78
  88.8 0.1 fusion.13
  88.9 0.1 copy.79
  89.0 0.2 reduce_window_sum.11
  89.2 0.1 copy.80
  89.3 0.1 reshape.96
  89.4 0.1 broadcast_in_dim.85
  89.5 0.2 broadcast_in_dim.86
  89.7 0.0 copy-done.6
  89.8 0.0 all-to-all-done
  89.8 3.2 reshape.125
  92.9 0.2 copy.95
  93.1 0.6 gather_fusion
  93.7 0.1 select_bitcast_fusion
  93.8 13.3 %gather_fusion.1 = bf16[384,176,32]{1,2,0:T(8,128)(2,1)} fusion(bf16[176,32,32]{0,2,1:T(8,128)(2,1)S(1)} %select_bitcast_fusion, s32[1024]{0:T(1024)S(1)} %pad_clamp_fusion), kind=kCustom, calls=%fused_computation.1 | custom fusion | bytes 8652288 | tf_op jit(solution)/shard_map/jit(_take)/gather | solution.py:46
  107.2 6.2 %broadcast_select_fusion = bf16[176,6,2048]{0,2,1:T(8,128)(2,1)S(1)} fusion(bf16[176,6,2048]{0,2,1:T(8,128)(2,1)} %bitcast.51, pred[6,2048]{1,0:T(8,128)(4,1)S(1)} %broadcast_in_dim.86), kind=kLoop, calls=%fused_computation.7 | loop fusion | flops 2162688 | bytes 8663040 | tf_op jit(solution)/shard_map/jit(_take)/select_n | solution.py:46
  113.4 22.3 %copy.82 = bf16[176,6,2048]{0,1,2:T(8,128)(2,1)} copy(bf16[176,6,2048]{0,2,1:T(8,128)(2,1)S(1)} %broadcast_select_fusion) | data formatting | bytes 8650752 | tf_op jit(solution)/shard_map/jit(_take)/select_n | solution.py:46
  135.7 8.6 %all-to-all-start.1 = ((bf16[176,6,2048]{0,1,2:T(8,128)(2,1)}), bf16[176,6,2048]{0,1,2:T(8,128)(2,1)}, u32[]{:S(2)}, u32[]{:S(2)}) async-start(bf16[176,6,2048]{0,1,2:T(8,128)(2,1)} %copy.82), calls=%async_computation.1 | async-start | bytes 16777216 | tf_op jit(solution)/shard_map/all_to_all | solution.py:47
  144.3 0.0 all-gather.4.cloned.1.call-start
  144.4 0.7 all-gather.4.cloned.1.call-update
  145.1 53.0 %all-gather.4.cloned.1.call-done = bf16[512,2048]{1,0:T(8,128)(2,1)} async-done(((bf16[512,256]{1,0:T(8,128)(2,1)}), bf16[512,2048]{1,0:T(8,128)(2,1)}) %all-gather.4.cloned.1.call-update) | async-done | bytes 2097168 | tf_op jit(solution)/shard_map/all_gather | solution.py:58
  198.0 0.0 copy-done.3
  198.0 2.1 fusion.2
  200.2 3.8 copy.87
  204.0 0.0 copy-start.5
  204.0 122.7 %all-to-all-done.1 = bf16[176,6,2048]{0,1,2:T(8,128)(2,1)} async-done(((bf16[176,6,2048]{0,1,2:T(8,128)(2,1)}), bf16[176,6,2048]{0,1,2:T(8,128)(2,1)}, u32[]{:S(2)}, u32[]{:S(2)}) %all-to-all-start.1) | async-done | bytes 4325408 | tf_op jit(solution)/shard_map/all_to_all | solution.py:47
  326.7 10.1 %all-to-all-start.2 = ((bf16[176,2,2048]{0,1,2:T(2,128)(2,1)}), bf16[176,2,2048]{0,1,2:T(2,128)(2,1)S(1)}, u32[]{:S(2)}, u32[]{:S(2)}) async-start(bf16[176,2,2048]{0,1,2:T(2,128)(2,1)} %copy.87), calls=%async_computation.3 | async-start | bytes 4194304 | tf_op jit(solution)/shard_map/all_to_all | solution.py:68
  336.8 0.0 reduce-scatter.2.cloned.1.call-start
  336.8 0.2 dynamic-slice_reduce_fusion
  337.0 0.0 copy-done.5
  337.0 0.1 select_reduce_fusion.2
  337.1 11.3 %copy.83 = bf16[176,6,2048]{2,0,1:T(8,128)(2,1)} copy(bf16[176,6,2048]{0,1,2:T(8,128)(2,1)} %all-to-all-done.1) | data formatting | bytes 8650752 | tf_op jit(solution)/shard_map/all_to_all | solution.py:47
  348.4 6.6 %convert_element_type.68 = f32[176,6,2048]{2,0,1:T(8,128)} convert(bf16[176,6,2048]{2,0,1:T(8,128)(2,1)} %copy.83) | non-fusion elementwise | flops 2162688 | bytes 12976128 | tf_op jit(solution)/shard_map/convert_element_type | solution.py:49
  355.0 4.8 multiply_reduce_fusion.1
  359.8 0.0 copy-start
  359.8 1.1 copy-done
  360.9 2.1 convolution_convert_fusion
  363.0 0.0 reduce-scatter.2.cloned.1.call-update
  363.0 53.9 %all-gather.1 = f32[64,2,4]{2,1,0:T(2,128)S(1)} all-gather(f32[1,2,4]{2,1,0:T(2,128)S(1)} %bitcast.66), channel_id=1, replica_groups=mesh['dp'=64,'tensor'=8] {'dp'}, dimensions={0}, use_global_device_ids=true | all-gather | bytes 2080 | tf_op jit(solution)/shard_map/all_gather | solution.py:36
  416.9 0.1 copy.90
  417.0 0.0 all-to-all-done.2
  417.0 0.6 bitcast_convert_fusion.1
  417.7 4.2 multiply_reduce_fusion
  421.9 3.7 fusion.3
  425.6 0.6 copy.92
  426.2 0.2 broadcast_in_dim.95
  426.4 1.6 scatter_fusion
  428.0 0.2 convert_element_type.80
  428.2 35.5 %all_to_all.31 = bf16[176,64,32]{0,2,1:T(8,128)(2,1)S(1)} all-to-all(bf16[176,64,32]{0,2,1:T(8,128)(2,1)S(1)} %convert_element_type.80), channel_id=1, replica_groups=mesh['dp'=64,'tensor'=8] {'dp'}, dimensions={1} | all-to-all | bytes 1441792 | tf_op jit(solution)/shard_map/all_to_all | solution.py:84
  463.7 1.5 bitcast_convert_fusion
  465.2 5.1 %copy.93 = f32[176,1,2048]{2,1,0:T(1,128)} copy(f32[176,1,2048]{0,2,1:T(8,128)} %bitcast_convert_fusion) | data formatting | bytes 2883584
  470.2 0.0 copy-done.1
  470.2 0.0 copy-done.2
  470.2 0.8 fusion.6
  471.1 0.7 copy.97
  (14 shorter events, 0.1 us)
Async XLA Ops:
  23.9 14.3 %copy-start.4 = (s32[2,4]{1,0:T(2,128)S(1)}, s32[2,4]{1,0:T(2,128)}, u32[]{:S(2)}) copy-start(s32[2,4]{1,0:T(2,128)} %param.9) | copy-start | bytes 100
  23.9 65.9 %copy-start.6 = (s32[32]{0:T(128)S(1)}, s32[32]{0:T(128)}, u32[]{:S(2)}) copy-start(s32[32]{0:T(128)} %param.11) | copy-start | bytes 388
  26.5 63.3 %all-to-all-start = ((bf16[64,2,2816]{2,1,0:T(2,128)(2,1)}), bf16[64,2,2816]{2,1,0:T(2,128)(2,1)S(1)}, u32[]{:S(2)}, u32[]{:S(2)}) async-start(bf16[64,2,2816]{2,1,0:T(2,128)(2,1)} %reshape.124), calls=%async_computation | async-start | bytes 1441792 | tf_op jit(solution)/shard_map/all_to_all | solution.py:44
  135.7 62.3 %copy-start.3 = (bf16[512,176]{0,1:T(8,128)(2,1)S(1)}, bf16[512,176]{0,1:T(8,128)(2,1)}, u32[]{:S(2)}) copy-start(bf16[512,176]{0,1:T(8,128)(2,1)} %param.6) | copy-start | bytes 540676
  135.7 191.0 %all-to-all-start.1 = ((bf16[176,6,2048]{0,1,2:T(8,128)(2,1)}), bf16[176,6,2048]{0,1,2:T(8,128)(2,1)}, u32[]{:S(2)}, u32[]{:S(2)}) async-start(bf16[176,6,2048]{0,1,2:T(8,128)(2,1)} %copy.82), calls=%async_computation.1 | async-start | bytes 16777216 | tf_op jit(solution)/shard_map/all_to_all | solution.py:47
  144.3 53.7 %all-gather.4.cloned.1.call-start = ((), (), s32[]{:S(2)}) async-start(), calls=%async_computation.6 | async-start | bytes 2359296 | tf_op jit(solution)/shard_map/all_gather | solution.py:58
  204.0 133.0 %copy-start.5 = (f32[2,4]{1,0:T(2,128)S(1)}, f32[2,4]{1,0:T(2,128)}, u32[]{:S(2)}) copy-start(f32[2,4]{1,0:T(2,128)} %param.10) | copy-start | bytes 100
  326.7 90.3 %all-to-all-start.2 = ((bf16[176,2,2048]{0,1,2:T(2,128)(2,1)}), bf16[176,2,2048]{0,1,2:T(2,128)(2,1)S(1)}, u32[]{:S(2)}, u32[]{:S(2)}) async-start(bf16[176,2,2048]{0,1,2:T(2,128)(2,1)} %copy.87), calls=%async_computation.3 | async-start | bytes 4194304 | tf_op jit(solution)/shard_map/all_to_all | solution.py:68
  336.8 135.0 %reduce-scatter.2.cloned.1.call-start = ((), (), s32[]{:S(2)}) async-start(), calls=%async_computation.5 | async-start | bytes 2359296 | tf_op jit(solution)/shard_map/reduce_scatter | solution.py:55
  359.8 1.1 copy-start
  465.2 5.1 %copy-start.1 = (bf16[176,2,2048]{2,0,1:T(8,128)(2,1)S(1)}, bf16[176,2,2048]{2,0,1:T(8,128)(2,1)}, u32[]{:S(2)}) copy-start(bf16[176,2,2048]{2,0,1:T(8,128)(2,1)} %copy-done) | copy-start | bytes 4325380
  465.2 5.1 %copy-start.2 = (bf16[512,2048]{1,0:T(8,128)(2,1)S(1)}, bf16[512,2048]{1,0:T(8,128)(2,1)}, u32[]{:S(2)}) copy-start(bf16[512,2048]{1,0:T(8,128)(2,1)} %all-gather.4.cloned.1.call-done) | copy-start | bytes 6291460
Sparse Core Ops, SparseCore 0:
  147.2 50.8 all-gather.3
  363.1 45.3 reduce-scatter.1
where the time goes:
time: 480 us; the launch traced here: 479 us
  waiting for transfers between devices  176 us (37%)
  blocking collectives  140 us (29%)
  local copies, waits for them, and re-layouts  72.6 us (15%)
  other arithmetic  36.2 us (8%)
  starting transfers between devices  30.4 us (6%)
  between operations  14.3 us (3%)
  matrix products  8.77 us (2%)
    all_to_all x1, waiting for transfers between devices, body(): lax.all_to_all(outgoing, 'dp', split_axis=2, concat_axis=2, tiled=True)  123 us
    all_gather x1, blocking collectives, body(): lax.all_gather(merge_weights, 'dp', axis=0, tiled=True)  53.9 us
    all_gather x1, waiting for transfers between devices, body(): full_cot = lax.all_gather(cotangent, 'tensor', axis=1, tiled=True)  53 us
    all_gather x1, blocking collectives, body(): lax.all_gather(expert_ids, 'dp', axis=0, tiled=True)  50.6 us
    all_to_all x1, blocking collectives, body(): lax.all_to_all(slotted.astype(jnp.bfloat16), 'dp', split_axis=1, concat_a...  35.5 us
    select_n x1, local copies, waits for them, and re-layouts, body(): jnp.take(by_expert, pools_all.T, axis=1).reshape(ff_local, POOL, width)  22.3 us
    unnamed x20, local copies, waits for them, and re-layouts  17.2 us
    gather x1, local copies, waits for them, and re-layouts, body(): jnp.take(by_expert, pools_all.T, axis=1).reshape(ff_local, POOL, width)  13.3 us
  transfers between devices with their start and end apart: 5, of which 2 were waited for; matrix products, arithmetic and copies ran while one was open for 11% of the time, Pallas kernels for 0%

commit v1 on v0

--- a/solution.py
+++ b/solution.py
@@ -55,7 +55,14 @@
     layer_out = lax.psum_scatter(
         partial_rows.astype(jnp.bfloat16), "tensor", scatter_dimension=1, tiled=True
     )
-    full_cot = lax.all_gather(cotangent, "tensor", axis=1, tiled=True)
+    ring = [cotangent]
+    for hop in range(7):
+        ring.append(lax.ppermute(ring[-1], "tensor", [(dev, (dev + 1) % 8) for dev in range(8)]))
+    full_cot = jnp.roll(
+        jnp.concatenate(ring[::-1], axis=1),
+        (lax.axis_index("tensor") + 1) * ring[0].shape[1],
+        axis=1,
+    )
     cot_seg = full_cot.reshape(seg_count, seg_len, width)
     grad_hidden = (
         jnp.einsum("std,fsd->stf", cot_seg, merged, preferred_element_type=jnp.float32)

time: 480 us -> 478 us (level)
  waiting for transfers between devices: 176 us -> 160 us
  starting transfers between devices: 30.4 us -> 45.8 us
    ppermute x0 -> x7, waiting for transfers between devices: none -> 55.2 us  [body(): lax.ppermute(ring[-1], 'tensor', [(dev, (dev + 1) % 8) for dev in range(8)])]
    all_gather x1 -> x0, waiting for transfers between devices: 53 us -> none  [body(): full_cot = lax.all_gather(cotangent, 'tensor', axis=1, tiled=True)]
    all_to_all x1, waiting for transfers between devices: 123 us -> 105 us  [body(): lax.all_to_all(outgoing, 'dp', split_axis=2, concat_axis=2, tiled=True)]
    ppermute x0 -> x7, starting transfers between devices: none -> 15.5 us  [body(): lax.ppermute(ring[-1], 'tensor', [(dev, (dev + 1) % 8) for dev in range(8)])]
    unnamed x20 -> x37, local copies, waits for them, and re-layouts: 17.2 us -> 17 us
  transfers between devices with their start and end apart: 5 -> 11, of which waited for: 2 -> 8; matrix products, arithmetic and copies ran while one was open for 11% -> 10% of each run, Pallas kernels for 0% -> 0%
where the time goes in v1:
time: 478 us; the launch traced here: 477 us
  waiting for transfers between devices  160 us (33%)
  blocking collectives  140 us (29%)
  local copies, waits for them, and re-layouts  72.6 us (15%)
  starting transfers between devices  45.8 us (10%)
  other arithmetic  34.9 us (7%)
  between operations  14.6 us (3%)
  matrix products  8.77 us (2%)
    all_to_all x1, waiting for transfers between devices, body(): lax.all_to_all(outgoing, 'dp', split_axis=2, concat_axis=2, tiled=True)  105 us
    ppermute x7, waiting for transfers between devices, body(): lax.ppermute(ring[-1], 'tensor', [(dev, (dev + 1) % 8) for dev in range(8)])  55.2 us
    all_gather x1, blocking collectives, body(): lax.all_gather(merge_weights, 'dp', axis=0, tiled=True)  53.9 us
    all_gather x1, blocking collectives, body(): lax.all_gather(expert_ids, 'dp', axis=0, tiled=True)  50.6 us
    all_to_all x1, blocking collectives, body(): lax.all_to_all(slotted.astype(jnp.bfloat16), 'dp', split_axis=1, concat_a...  35.7 us
    select_n x1, local copies, waits for them, and re-layouts, body(): jnp.take(by_expert, pools_all.T, axis=1).reshape(ff_local, POOL, width)  22.3 us
    unnamed x37, local copies, waits for them, and re-layouts  17 us
    ppermute x7, starting transfers between devices, body(): lax.ppermute(ring[-1], 'tensor', [(dev, (dev + 1) % 8) for dev in range(8)])  15.5 us
  transfers between devices with their start and end apart: 11, of which 8 were waited for; matrix products, arithmetic and copies ran while one was open for 10% of the time, Pallas kernels for 0%

profile of v1, /device:TPU:1, one launch (start us, length us, event | category | flops | bytes accessed | tf_op | source)
XLA Modules:
  0.0 477.1 jit_solution(12074160636776424067)
XLA Ops:
  7.2 4.5 copy.81
  11.7 0.5 broadcast.43
  12.3 11.6 %reduce.2 = bf16[2048,176]{1,0:T(8,128)(2,1)S(1)} reduce(bf16[2048,1,176]{2,1,0:T(2,128)(2,1)S(1)} %bitcast.54, bf16[]{:T(256)} %broadcast.43), dimensions={1}, to_apply=%bitcast.43.reduce_sub_computation | reduce | bytes 1441794
  23.9 2.6 reshape.124
  26.5 11.6 %all-to-all-start = ((bf16[64,2,2816]{2,1,0:T(2,128)(2,1)}), bf16[64,2,2816]{2,1,0:T(2,128)(2,1)S(1)}, u32[]{:S(2)}, u32[]{:S(2)}) async-start(bf16[64,2,2816]{2,1,0:T(2,128)(2,1)} %reshape.124), calls=%async_computation | async-start | bytes 1441792 | tf_op jit(solution)/shard_map/all_to_all | solution.py:44
  38.1 50.6 %all-gather = s32[64,2,4]{2,1,0:T(2,128)S(1)} all-gather(s32[1,2,4]{2,1,0:T(2,128)S(1)} %bitcast.64), channel_id=1, replica_groups=mesh['dp'=64,'tensor'=8] {'dp'}, dimensions={0}, use_global_device_ids=true | all-gather | bytes 2080 | tf_op jit(solution)/shard_map/all_gather | solution.py:35
  88.8 0.1 copy.78
  88.8 0.1 fusion.13
  88.9 0.1 copy.79
  89.0 0.2 reduce_window_sum.11
  89.2 0.1 copy.80
  89.3 0.1 reshape.96
  89.4 0.1 broadcast_in_dim.85
  89.5 0.2 broadcast_in_dim.86
  89.8 3.2 reshape.125
  93.0 0.2 copy.95
  93.1 0.6 gather_fusion
  93.7 0.1 select_bitcast_fusion
  93.9 13.3 %gather_fusion.1 = bf16[384,176,32]{1,2,0:T(8,128)(2,1)} fusion(bf16[176,32,32]{0,2,1:T(8,128)(2,1)S(1)} %select_bitcast_fusion, s32[1024]{0:T(1024)S(1)} %pad_clamp_fusion), kind=kCustom, calls=%fused_computation.1 | custom fusion | bytes 8652288 | tf_op jit(solution)/shard_map/jit(_take)/gather | solution.py:46
  107.2 6.2 %broadcast_select_fusion = bf16[176,6,2048]{0,2,1:T(8,128)(2,1)S(1)} fusion(bf16[176,6,2048]{0,2,1:T(8,128)(2,1)} %bitcast.50, pred[6,2048]{1,0:T(8,128)(4,1)S(1)} %broadcast_in_dim.86), kind=kLoop, calls=%fused_computation.7 | loop fusion | flops 2162688 | bytes 8663040 | tf_op jit(solution)/shard_map/jit(_take)/select_n | solution.py:46
  113.4 22.3 %copy.82 = bf16[176,6,2048]{0,1,2:T(8,128)(2,1)} copy(bf16[176,6,2048]{0,2,1:T(8,128)(2,1)S(1)} %broadcast_select_fusion) | data formatting | bytes 8650752 | tf_op jit(solution)/shard_map/jit(_take)/select_n | solution.py:46
  135.7 8.6 %all-to-all-start.1 = ((bf16[176,6,2048]{0,1,2:T(8,128)(2,1)}), bf16[176,6,2048]{0,1,2:T(8,128)(2,1)}, u32[]{:S(2)}, u32[]{:S(2)}) async-start(bf16[176,6,2048]{0,1,2:T(8,128)(2,1)} %copy.82), calls=%async_computation.1 | async-start | bytes 16777216 | tf_op jit(solution)/shard_map/all_to_all | solution.py:47
  144.3 4.0 collective-permute-start
  148.3 13.0 %collective-permute-done = bf16[512,256]{1,0:T(8,128)(2,1)S(1)} collective-permute-done((bf16[512,256]{1,0:T(8,128)(2,1)S(1)}, bf16[512,256]{1,0:T(8,128)(2,1)S(1)}, u32[]{:S(2)}, u32[]{:S(2)}) %collective-permute-start) | collective-permute-done | bytes 262176 | tf_op jit(solution)/shard_map/ppermute | solution.py:60
  161.3 1.9 collective-permute-start.1
  163.2 8.1 %collective-permute-done.1 = bf16[512,256]{1,0:T(8,128)(2,1)S(1)} collective-permute-done((bf16[512,256]{1,0:T(8,128)(2,1)S(1)}, bf16[512,256]{1,0:T(8,128)(2,1)S(1)}, u32[]{:S(2)}, u32[]{:S(2)}) %collective-permute-start.1) | collective-permute-done | bytes 262176 | tf_op jit(solution)/shard_map/ppermute | solution.py:60
  171.3 1.9 collective-permute-start.2
  173.3 7.3 %collective-permute-done.2 = bf16[512,256]{1,0:T(8,128)(2,1)S(1)} collective-permute-done((bf16[512,256]{1,0:T(8,128)(2,1)S(1)}, bf16[512,256]{1,0:T(8,128)(2,1)S(1)}, u32[]{:S(2)}, u32[]{:S(2)}) %collective-permute-start.2) | collective-permute-done | bytes 262176 | tf_op jit(solution)/shard_map/ppermute | solution.py:60
  180.6 1.9 collective-permute-start.3
  182.5 6.8 %collective-permute-done.3 = bf16[512,256]{1,0:T(8,128)(2,1)S(1)} collective-permute-done((bf16[512,256]{1,0:T(8,128)(2,1)S(1)}, bf16[512,256]{1,0:T(8,128)(2,1)S(1)}, u32[]{:S(2)}, u32[]{:S(2)}) %collective-permute-start.3) | collective-permute-done | bytes 262176 | tf_op jit(solution)/shard_map/ppermute | solution.py:60
  189.3 1.9 collective-permute-start.4
  191.2 6.8 %collective-permute-done.4 = bf16[512,256]{1,0:T(8,128)(2,1)S(1)} collective-permute-done((bf16[512,256]{1,0:T(8,128)(2,1)S(1)}, bf16[512,256]{1,0:T(8,128)(2,1)S(1)}, u32[]{:S(2)}, u32[]{:S(2)}) %collective-permute-start.4) | collective-permute-done | bytes 262176 | tf_op jit(solution)/shard_map/ppermute | solution.py:60
  198.0 1.9 collective-permute-start.5
  199.9 6.8 %collective-permute-done.5 = bf16[512,256]{1,0:T(8,128)(2,1)S(1)} collective-permute-done((bf16[512,256]{1,0:T(8,128)(2,1)S(1)}, bf16[512,256]{1,0:T(8,128)(2,1)S(1)}, u32[]{:S(2)}, u32[]{:S(2)}) %collective-permute-start.5) | collective-permute-done | bytes 262176 | tf_op jit(solution)/shard_map/ppermute | solution.py:60
  206.7 1.9 collective-permute-start.6
  208.7 6.4 %collective-permute-done.6 = bf16[512,256]{1,0:T(8,128)(2,1)S(1)} collective-permute-done((bf16[512,256]{1,0:T(8,128)(2,1)S(1)}, bf16[512,256]{1,0:T(8,128)(2,1)S(1)}, u32[]{:S(2)}, u32[]{:S(2)}) %collective-permute-start.6) | collective-permute-done | bytes 262176 | tf_op jit(solution)/shard_map/ppermute | solution.py:60
  215.6 0.2 constant_dynamic-slice_fusion
  215.9 1.3 copy-done
  217.2 0.5 fusion.2
  217.8 3.8 copy.87
  221.6 105.1 %all-to-all-done.1 = bf16[176,6,2048]{0,1,2:T(8,128)(2,1)} async-done(((bf16[176,6,2048]{0,1,2:T(8,128)(2,1)}), bf16[176,6,2048]{0,1,2:T(8,128)(2,1)}, u32[]{:S(2)}, u32[]{:S(2)}) %all-to-all-start.1) | async-done | bytes 4325408 | tf_op jit(solution)/shard_map/all_to_all | solution.py:47
  326.7 10.1 %all-to-all-start.2 = ((bf16[176,2,2048]{0,1,2:T(2,128)(2,1)}), bf16[176,2,2048]{0,1,2:T(2,128)(2,1)S(1)}, u32[]{:S(2)}, u32[]{:S(2)}) async-start(bf16[176,2,2048]{0,1,2:T(2,128)(2,1)} %copy.87), calls=%async_computation.3 | async-start | bytes 4194304 | tf_op jit(solution)/shard_map/all_to_all | solution.py:75
  336.8 0.0 reduce-scatter.2.cloned.1.call-start
  336.8 0.2 dynamic-slice_reduce_fusion
  337.0 0.1 select_reduce_fusion.2
  337.1 11.3 %copy.83 = bf16[176,6,2048]{2,0,1:T(8,128)(2,1)} copy(bf16[176,6,2048]{0,1,2:T(8,128)(2,1)} %all-to-all-done.1) | data formatting | bytes 8650752 | tf_op jit(solution)/shard_map/all_to_all | solution.py:47
  348.4 6.6 %convert_element_type.65 = f32[176,6,2048]{2,0,1:T(8,128)} convert(bf16[176,6,2048]{2,0,1:T(8,128)(2,1)} %copy.83) | non-fusion elementwise | flops 2162688 | bytes 12976128 | tf_op jit(solution)/shard_map/convert_element_type | solution.py:49
  355.0 4.8 multiply_reduce_fusion.1
  359.8 1.1 copy-done.1
  360.9 2.1 convolution_convert_fusion
  363.0 53.9 %all-gather.1 = f32[64,2,4]{2,1,0:T(2,128)S(1)} all-gather(f32[1,2,4]{2,1,0:T(2,128)S(1)} %bitcast.65), channel_id=1, replica_groups=mesh['dp'=64,'tensor'=8] {'dp'}, dimensions={0}, use_global_device_ids=true | all-gather | bytes 2080 | tf_op jit(solution)/shard_map/all_gather | solution.py:36
  416.9 0.1 copy.90
  417.0 0.6 bitcast_convert_fusion.1
  417.7 4.2 multiply_reduce_fusion
  421.9 3.7 fusion.3
  425.6 0.6 copy.92
  426.2 0.2 broadcast_in_dim.95
  426.4 1.6 scatter_fusion
  428.0 0.2 convert_element_type.76
  428.2 35.7 %all_to_all.31 = bf16[176,64,32]{0,2,1:T(8,128)(2,1)S(1)} all-to-all(bf16[176,64,32]{0,2,1:T(8,128)(2,1)S(1)} %convert_element_type.76), channel_id=1, replica_groups=mesh['dp'=64,'tensor'=8] {'dp'}, dimensions={1} | all-to-all | bytes 1441792 | tf_op jit(solution)/shard_map/all_to_all | solution.py:91
  463.9 0.2 bitcast_convert_fusion
  464.0 3.1 copy.93
  467.1 2.4 fusion.6
  469.6 0.7 copy.97
  (44 shorter events, 0.6 us)
Async XLA Ops:
  7.2 31.0 %copy-start.5 = (s32[2,4]{1,0:T(2,128)S(1)}, s32[2,4]{1,0:T(2,128)}, u32[]{:S(2)}) copy-start(s32[2,4]{1,0:T(2,128)} %param.9) | copy-start | bytes 100
  7.2 82.5 %copy-start.7 = (s32[32]{0:T(128)S(1)}, s32[32]{0:T(128)}, u32[]{:S(2)}) copy-start(s32[32]{0:T(128)} %param.11) | copy-start | bytes 388
  26.5 63.3 %all-to-all-start = ((bf16[64,2,2816]{2,1,0:T(2,128)(2,1)}), bf16[64,2,2816]{2,1,0:T(2,128)(2,1)S(1)}, u32[]{:S(2)}, u32[]{:S(2)}) async-start(bf16[64,2,2816]{2,1,0:T(2,128)(2,1)} %reshape.124), calls=%async_computation | async-start | bytes 1441792 | tf_op jit(solution)/shard_map/all_to_all | solution.py:44
  135.7 8.6 %copy-start.3 = (bf16[512,256]{1,0:T(8,128)(2,1)S(1)}, bf16[512,256]{1,0:T(8,128)(2,1)}, u32[]{:S(2)}) copy-start(bf16[512,256]{1,0:T(8,128)(2,1)} %param.7) | copy-start | bytes 786436
  135.7 191.0 %all-to-all-start.1 = ((bf16[176,6,2048]{0,1,2:T(8,128)(2,1)}), bf16[176,6,2048]{0,1,2:T(8,128)(2,1)}, u32[]{:S(2)}, u32[]{:S(2)}) async-start(bf16[176,6,2048]{0,1,2:T(8,128)(2,1)} %copy.82), calls=%async_computation.1 | async-start | bytes 16777216 | tf_op jit(solution)/shard_map/all_to_all | solution.py:47
  144.3 17.0 %collective-permute-start = (bf16[512,256]{1,0:T(8,128)(2,1)S(1)}, bf16[512,256]{1,0:T(8,128)(2,1)S(1)}, u32[]{:S(2)}, u32[]{:S(2)}) collective-permute-start(bf16[512,256]{1,0:T(8,128)(2,1)S(1)} %copy-done.3), channel_id=1, source_target_pairs={{0,1},{1,2},{2,3},{3,4},{4,5},{5,6},{6,7},{7,0},{8,9},{9,10},{10,1... | collective-permute-start | bytes 786440 | tf_op jit(solution)/shard_map/ppermute | solution.py:60
  161.3 10.0 %collective-permute-start.1 = (bf16[512,256]{1,0:T(8,128)(2,1)S(1)}, bf16[512,256]{1,0:T(8,128)(2,1)S(1)}, u32[]{:S(2)}, u32[]{:S(2)}) collective-permute-start(bf16[512,256]{1,0:T(8,128)(2,1)S(1)} %collective-permute-done), channel_id=1, source_target_pairs={{0,1},{1,2},{2,3},{3,4},{4,5},{5,6},{6,7},{7,0},{8,9},{9,10},{10,1... | collective-permute-start | bytes 786440 | tf_op jit(solution)/shard_map/ppermute | solution.py:60
  171.3 9.2 %collective-permute-start.2 = (bf16[512,256]{1,0:T(8,128)(2,1)S(1)}, bf16[512,256]{1,0:T(8,128)(2,1)S(1)}, u32[]{:S(2)}, u32[]{:S(2)}) collective-permute-start(bf16[512,256]{1,0:T(8,128)(2,1)S(1)} %collective-permute-done.1), channel_id=1, source_target_pairs={{0,1},{1,2},{2,3},{3,4},{4,5},{5,6},{6,7},{7,0},{8,9},{9,10},{10,1... | collective-permute-start | bytes 786440 | tf_op jit(solution)/shard_map/ppermute | solution.py:60
  180.6 8.7 %collective-permute-start.3 = (bf16[512,256]{1,0:T(8,128)(2,1)S(1)}, bf16[512,256]{1,0:T(8,128)(2,1)S(1)}, u32[]{:S(2)}, u32[]{:S(2)}) collective-permute-start(bf16[512,256]{1,0:T(8,128)(2,1)S(1)} %collective-permute-done.2), channel_id=1, source_target_pairs={{0,1},{1,2},{2,3},{3,4},{4,5},{5,6},{6,7},{7,0},{8,9},{9,10},{10,1... | collective-permute-start | bytes 786440 | tf_op jit(solution)/shard_map/ppermute | solution.py:60
  189.3 8.7 %collective-permute-start.4 = (bf16[512,256]{1,0:T(8,128)(2,1)S(1)}, bf16[512,256]{1,0:T(8,128)(2,1)S(1)}, u32[]{:S(2)}, u32[]{:S(2)}) collective-permute-start(bf16[512,256]{1,0:T(8,128)(2,1)S(1)} %collective-permute-done.3), channel_id=1, source_target_pairs={{0,1},{1,2},{2,3},{3,4},{4,5},{5,6},{6,7},{7,0},{8,9},{9,10},{10,1... | collective-permute-start | bytes 786440 | tf_op jit(solution)/shard_map/ppermute | solution.py:60
  198.0 8.7 %collective-permute-start.5 = (bf16[512,256]{1,0:T(8,128)(2,1)S(1)}, bf16[512,256]{1,0:T(8,128)(2,1)S(1)}, u32[]{:S(2)}, u32[]{:S(2)}) collective-permute-start(bf16[512,256]{1,0:T(8,128)(2,1)S(1)} %collective-permute-done.4), channel_id=1, source_target_pairs={{0,1},{1,2},{2,3},{3,4},{4,5},{5,6},{6,7},{7,0},{8,9},{9,10},{10,1... | collective-permute-start | bytes 786440 | tf_op jit(solution)/shard_map/ppermute | solution.py:60
  206.7 8.3 %collective-permute-start.6 = (bf16[512,256]{1,0:T(8,128)(2,1)S(1)}, bf16[512,256]{1,0:T(8,128)(2,1)S(1)}, u32[]{:S(2)}, u32[]{:S(2)}) collective-permute-start(bf16[512,256]{1,0:T(8,128)(2,1)S(1)} %collective-permute-done.5), channel_id=1, source_target_pairs={{0,1},{1,2},{2,3},{3,4},{4,5},{5,6},{6,7},{7,0},{8,9},{9,10},{10,1... | collective-permute-start | bytes 786440 | tf_op jit(solution)/shard_map/ppermute | solution.py:60
  215.3 1.9 copy-start.4
  215.9 1.4 copy-start
  217.8 119.2 %copy-start.6 = (f32[2,4]{1,0:T(2,128)S(1)}, f32[2,4]{1,0:T(2,128)}, u32[]{:S(2)}) copy-start(f32[2,4]{1,0:T(2,128)} %param.10) | copy-start | bytes 100
  326.7 90.3 %all-to-all-start.2 = ((bf16[176,2,2048]{0,1,2:T(2,128)(2,1)}), bf16[176,2,2048]{0,1,2:T(2,128)(2,1)S(1)}, u32[]{:S(2)}, u32[]{:S(2)}) async-start(bf16[176,2,2048]{0,1,2:T(2,128)(2,1)} %copy.87), calls=%async_computation.3 | async-start | bytes 4194304 | tf_op jit(solution)/shard_map/all_to_all | solution.py:75
  336.8 133.5 %reduce-scatter.2.cloned.1.call-start = ((), (), s32[]{:S(2)}) async-start(), calls=%async_computation.5 | async-start | bytes 2359296 | tf_op jit(solution)/shard_map/reduce_scatter | solution.py:55
  359.8 1.1 copy-start.1
  428.2 38.9 %copy-start.2 = (bf16[176,2,2048]{2,0,1:T(8,128)(2,1)S(1)}, bf16[176,2,2048]{2,0,1:T(8,128)(2,1)}, u32[]{:S(2)}) copy-start(bf16[176,2,2048]{2,0,1:T(8,128)(2,1)} %copy-done.1) | copy-start | bytes 4325380
Sparse Core Ops, SparseCore 0:
  363.1 45.3 reduce-scatter.1
